TPU v7x, 256 devices: a whole 4x4x8 slice. The times are simulated.
256 devices in a mesh: wide: 16 (over z_hi, x), narrow: 16 (over z_lo, y, core).
Axes of the slice: x: 4, y: 4, z: 8 (z_hi: 4, z_lo: 2; z = z_hi * 2 + z_lo), core: 2. Of those that a mesh axis runs over, the one named last changes fastest.
Arguments:
- node: bfloat16 [256, 256, 256], P('narrow'), may hold values from -6 to 6
- right_side: bfloat16 [256, 256, 256], P('narrow'), may hold values from -16 to 16
- leg_ops: bfloat16 [3, 12, 256, 256], replicated, may hold values from -0.375 to 0.375
- op_index: int32 [64, 3], P('wide'), may hold values from 0 to 11, as said below
- offsets: int32 [64], P('wide'), may hold values from 0 to 7
Outputs:
- new_node: float32 [256, 256, 256], P('narrow')
Inputs may be any that keep to these rules, and one draw needn't show every extreme that they name: `op_index`: no two triples name the same pair of leg b and leg c operators; every operator of each leg is named by some triple.
All inputs are finite; a program needn't handle non-finite values.
Results may differ from a plain program's by a relative error of at most 0.0019.
Values may be sent and summed in bfloat16 or wider, within the bound.
No kernel may reach another device: no remote copies, remote signals or barrier semaphores. Data moves between devices by JAX's collectives and lax.ppermute only.
A program may use at most 64 MiB of HBM per device.

v0:
```python
import math
import jax
import jax.numpy as jnp
from jax import lax
from jax.sharding import PartitionSpec as P

SECTORS = 8


def two_legs(rounded, leg_ops, op_index, triple):
    op_b = leg_ops[1, op_index[triple, 1]]
    op_c = leg_ops[2, op_index[triple, 2]]
    first = jnp.einsum("abc,qc->abq", rounded, op_c, preferred_element_type=jnp.float32).astype(
        jnp.bfloat16
    )
    return jnp.einsum("pb,abq->paq", op_b, first, preferred_element_type=jnp.float32).astype(
        jnp.bfloat16
    )


def third_leg(regrouped, leg_ops, op_index, offsets, triple, sector):
    op_a = jnp.roll(leg_ops[0, op_index[triple, 0]], offsets[triple] * sector, axis=0)
    return jnp.einsum("ra,paq->rpq", op_a, regrouped, preferred_element_type=jnp.float32)


def per_device(node, right_side, leg_ops, op_index, offsets):
    bond = node.shape[1]
    sector = bond // SECTORS
    trip_local = op_index.shape[0]
    tau = 0.5 / math.sqrt(trip_local * lax.axis_size("wide"))
    partial_value = None
    for triple in range(trip_local):
        second = two_legs(node, leg_ops, op_index, triple)
        regrouped = lax.all_to_all(second, "narrow", split_axis=0, concat_axis=1, tiled=True)
        term = third_leg(regrouped, leg_ops, op_index, offsets, triple, sector)
        partial_value = term if partial_value is None else partial_value + term
    back = lax.all_to_all(partial_value, "narrow", split_axis=0, concat_axis=1, tiled=True)
    sigma = lax.psum(back, "wide")
    return node.astype(jnp.float32) + tau * (right_side.astype(jnp.float32) - sigma)


def solution(mesh):
    in_specs = (P("narrow", None, None), P("narrow", None, None), P(), P("wide", None), P("wide"))
    out_specs = P("narrow", None, None)
    return jax.shard_map(
        per_device, mesh=mesh, in_specs=in_specs, out_specs=out_specs, check_vma=False
    )
```

profile of v0, /device:TPU:8, one launch (start us, length us, event | category | flops | bytes accessed | tf_op | source)
XLA Modules:
  0.0 456.6 jit_solution(17279808986567162240)
XLA Ops:
  6.5 1.8 fusion.99
  12.3 3.2 fusion.26
  15.5 2.5 copy.15
  18.0 6.5 %all-to-all-start.2 = ((bf16[256,16,256]{2,1,0:T(8,128)(2,1)}), bf16[256,16,256]{2,1,0:T(8,128)(2,1)}, u32[]{:S(2)}, u32[]{:S(2)}) async-start(bf16[256,16,256]{2,1,0:T(8,128)(2,1)} %copy.15), calls=%async_computation.2 | async-start | bytes 4194304 | tf_op jit(solution)/shard_map/all_to_all | solution.py:34
  28.1 3.8 fusion.23
  31.8 4.1 copy.13
  36.0 15.6 %all-to-all-done.2 = bf16[256,16,256]{2,1,0:T(8,128)(2,1)} async-done(((bf16[256,16,256]{2,1,0:T(8,128)(2,1)}), bf16[256,16,256]{2,1,0:T(8,128)(2,1)}, u32[]{:S(2)}, u32[]{:S(2)}) %all-to-all-start.2) | async-done | bytes 2097184 | tf_op jit(solution)/shard_map/all_to_all | solution.py:34
  51.6 6.8 %all-to-all-start.1 = ((bf16[256,16,256]{2,1,0:T(8,128)(2,1)}), bf16[256,16,256]{2,1,0:T(8,128)(2,1)}, u32[]{:S(2)}, u32[]{:S(2)}) async-start(bf16[256,16,256]{2,1,0:T(8,128)(2,1)} %copy.13), calls=%async_computation.1 | async-start | bytes 4194304 | tf_op jit(solution)/shard_map/all_to_all | solution.py:34
  62.1 3.8 fusion.20
  65.9 4.1 copy.11
  70.0 15.5 %all-to-all-done.1 = bf16[256,16,256]{2,1,0:T(8,128)(2,1)} async-done(((bf16[256,16,256]{2,1,0:T(8,128)(2,1)}), bf16[256,16,256]{2,1,0:T(8,128)(2,1)}, u32[]{:S(2)}, u32[]{:S(2)}) %all-to-all-start.1) | async-done | bytes 2097184 | tf_op jit(solution)/shard_map/all_to_all | solution.py:34
  85.5 6.8 %all-to-all-start = ((bf16[256,16,256]{2,1,0:T(8,128)(2,1)}), bf16[256,16,256]{2,1,0:T(8,128)(2,1)}, u32[]{:S(2)}, u32[]{:S(2)}) async-start(bf16[256,16,256]{2,1,0:T(8,128)(2,1)} %copy.11), calls=%async_computation | async-start | bytes 4194304 | tf_op jit(solution)/shard_map/all_to_all | solution.py:34
  95.9 3.8 fusion.29
  99.6 4.1 copy.17
  103.8 15.7 %all-to-all-done = bf16[256,16,256]{2,1,0:T(8,128)(2,1)} async-done(((bf16[256,16,256]{2,1,0:T(8,128)(2,1)}), bf16[256,16,256]{2,1,0:T(8,128)(2,1)}, u32[]{:S(2)}, u32[]{:S(2)}) %all-to-all-start) | async-done | bytes 2097184 | tf_op jit(solution)/shard_map/all_to_all | solution.py:34
  119.5 6.8 %all-to-all-start.3 = ((bf16[256,16,256]{2,1,0:T(8,128)(2,1)}), bf16[256,16,256]{2,1,0:T(8,128)(2,1)}, u32[]{:S(2)}, u32[]{:S(2)}) async-start(bf16[256,16,256]{2,1,0:T(8,128)(2,1)} %copy.17), calls=%async_computation.3 | async-start | bytes 4194304 | tf_op jit(solution)/shard_map/all_to_all | solution.py:34
  137.3 1.1 dynamic-slice_bitcast_fusion
  138.4 3.1 copy.16
  141.6 3.1 copy.14
  144.7 3.1 copy.12
  147.9 5.6 %all-to-all-done.3 = bf16[256,16,256]{2,1,0:T(8,128)(2,1)} async-done(((bf16[256,16,256]{2,1,0:T(8,128)(2,1)}), bf16[256,16,256]{2,1,0:T(8,128)(2,1)}, u32[]{:S(2)}, u32[]{:S(2)}) %all-to-all-start.3) | async-done | bytes 2097184 | tf_op jit(solution)/shard_map/all_to_all | solution.py:34
  153.5 1.9 copy.18
  155.7 0.9 fusion.37
  156.6 0.7 copy-done.2
  157.3 0.9 fusion.41
  158.9 0.9 fusion.45
  159.7 1.1 add_add_fusion
  160.9 2.4 copy.19
  163.3 53.1 %all_to_all.90 = f32[256,16,256]{2,1,0:T(8,128)S(1)} all-to-all(f32[256,16,256]{2,1,0:T(8,128)S(1)} %copy.19), channel_id=1, replica_groups=mesh['wide'=16,'narrow'=16] {'narrow'}, dimensions={0} | all-to-all | bytes 8388608 | tf_op jit(solution)/shard_map/all_to_all | solution.py:37
  216.4 2.6 copy.20
  219.1 225.0 %all-reduce.2.cloned.1.call-done = f32[16,256,256]{2,1,0:T(8,128)} async-done(((f32[16,256,256]{2,1,0:T(8,128)}), f32[16,256,256]{2,1,0:T(8,128)}) %all-reduce.2.cloned.1.call-update) | async-done | bytes 4194320 | tf_op jit(solution)/shard_map/psum | solution.py:38
  444.1 5.7 %multiply_add_fusion = f32[16,256,256]{2,1,0:T(8,128)} fusion(f32[16,256,256]{2,1,0:T(8,128)} %all-reduce.2.cloned.1.call-done, bf16[16,256,256]{2,1,0:T(8,128)(2,1)} %param.8, bf16[16,256,256]{2,1,0:T(8,128)(2,1)S(1)} %copy-done), kind=kLoop, calls=%fused_computation | loop fusion | flops 5242880 | bytes 12582912 | tf_op jit(solution)/shard_map/add | solution.py:39
  (12 shorter events, 1.9 us)
Async XLA Ops:
  18.0 10.1 %copy-start = (bf16[16,256,256]{2,1,0:T(8,128)(2,1)S(1)}, bf16[16,256,256]{2,1,0:T(8,128)(2,1)}, u32[]{:S(2)}) copy-start(bf16[16,256,256]{2,1,0:T(8,128)(2,1)} %param.7) | copy-start | bytes 6291460
  18.0 33.5 %all-to-all-start.2 = ((bf16[256,16,256]{2,1,0:T(8,128)(2,1)}), bf16[256,16,256]{2,1,0:T(8,128)(2,1)}, u32[]{:S(2)}, u32[]{:S(2)}) async-start(bf16[256,16,256]{2,1,0:T(8,128)(2,1)} %copy.15), calls=%async_computation.2 | async-start | bytes 4194304 | tf_op jit(solution)/shard_map/all_to_all | solution.py:34
  51.6 34.0 %all-to-all-start.1 = ((bf16[256,16,256]{2,1,0:T(8,128)(2,1)}), bf16[256,16,256]{2,1,0:T(8,128)(2,1)}, u32[]{:S(2)}, u32[]{:S(2)}) async-start(bf16[256,16,256]{2,1,0:T(8,128)(2,1)} %copy.13), calls=%async_computation.1 | async-start | bytes 4194304 | tf_op jit(solution)/shard_map/all_to_all | solution.py:34
  85.5 34.0 %all-to-all-start = ((bf16[256,16,256]{2,1,0:T(8,128)(2,1)}), bf16[256,16,256]{2,1,0:T(8,128)(2,1)}, u32[]{:S(2)}, u32[]{:S(2)}) async-start(bf16[256,16,256]{2,1,0:T(8,128)(2,1)} %copy.11), calls=%async_computation | async-start | bytes 4194304 | tf_op jit(solution)/shard_map/all_to_all | solution.py:34
  103.8 22.7 %copy-start.4 = (s32[4]{0:T(128)S(1)}, s32[4]{0:T(128)}, u32[]{:S(2)}) copy-start(s32[4]{0:T(128)} %param.11) | copy-start | bytes 52
  119.5 34.0 %all-to-all-start.3 = ((bf16[256,16,256]{2,1,0:T(8,128)(2,1)}), bf16[256,16,256]{2,1,0:T(8,128)(2,1)}, u32[]{:S(2)}, u32[]{:S(2)}) async-start(bf16[256,16,256]{2,1,0:T(8,128)(2,1)} %copy.17), calls=%async_computation.3 | async-start | bytes 4194304 | tf_op jit(solution)/shard_map/all_to_all | solution.py:34
  126.3 317.8 %all-reduce.2.cloned.1.call-start = ((), (), s32[]{:S(2)}) async-start(), calls=%async_computation.5 | async-start | bytes 8388608 | tf_op jit(solution)/shard_map/psum | solution.py:38
  153.4 2.2 copy-start.3
  155.7 1.6 copy-start.2
  157.3 1.6 copy-start.1
Sparse Core Ops, SparseCore 0:
  219.2 224.8 all-reduce.1
where the time goes:
time: 458 us; the launch traced here: 457 us
  waiting for transfers between devices  277 us (60%)
  blocking collectives  53.1 us (12%)
  between operations  38.6 us (8%)
  local copies, waits for them, and re-layouts  36.6 us (8%)
  starting transfers between devices  27 us (6%)
  matrix products  18.2 us (4%)
  other arithmetic  5.71 us (1%)
    psum x1, waiting for transfers between devices, per_device(): sigma = lax.psum(back, 'wide')  225 us
    all_to_all x1, blocking collectives, per_device(): lax.all_to_all(partial_value, 'narrow', split_axis=0, concat_axis=1, tile...  53.1 us
    all_to_all x4, waiting for transfers between devices, per_device(): lax.all_to_all(second, 'narrow', split_axis=0, concat_axis=1, tiled=True)  52.4 us
    all_to_all x4, starting transfers between devices, per_device(): lax.all_to_all(second, 'narrow', split_axis=0, concat_axis=1, tiled=True)  26.8 us
    convert_element_type x4, local copies, waits for them, and re-layouts, two_legs(): jnp.einsum('pb,abq->paq', op_b, first, preferred_element_type=jnp.float32)  14.9 us
    dot_general x4, matrix products, two_legs(): jnp.einsum('pb,abq->paq', op_b, first, preferred_element_type=jnp.float32)  14.5 us
    all_to_all x4, local copies, waits for them, and re-layouts, per_device(): lax.all_to_all(second, 'narrow', split_axis=0, concat_axis=1, tiled=True)  11.4 us
  transfers between devices with their start and end apart: 5, of which 5 were waited for; matrix products, arithmetic and copies ran while one was open for 8% of the time, Pallas kernels for 0%

commit v1 on v0

--- a/solution.py
+++ b/solution.py
@@ -34,7 +34,12 @@
         regrouped = lax.all_to_all(second, "narrow", split_axis=0, concat_axis=1, tiled=True)
         term = third_leg(regrouped, leg_ops, op_index, offsets, triple, sector)
         partial_value = term if partial_value is None else partial_value + term
-    back = lax.all_to_all(partial_value, "narrow", split_axis=0, concat_axis=1, tiled=True)
+    back = jnp.concatenate(
+        jax.lax.all_to_all(
+            jnp.stack(jnp.split(partial_value, jax.lax.psum(1, "narrow"), 0), 0), "narrow", 0, 0
+        ),
+        1,
+    )
     sigma = lax.psum(back, "wide")
     return node.astype(jnp.float32) + tau * (right_side.astype(jnp.float32) - sigma)
 

time: 458 us -> 460 us (level)
  no operation moved by 1% of the time
where the time goes in v1:
time: 460 us; the launch traced here: 459 us
  waiting for transfers between devices  277 us (60%)
  blocking collectives  53.1 us (12%)
  between operations  38.9 us (8%)
  local copies, waits for them, and re-layouts  37.5 us (8%)
  starting transfers between devices  26.9 us (6%)
  matrix products  19.5 us (4%)
  other arithmetic  5.71 us (1%)
    psum x1, waiting for transfers between devices, per_device(): sigma = lax.psum(back, 'wide')  225 us
    all_to_all x1, blocking collectives, per_device(): jax.lax.all_to_all(jnp.stack(jnp.split(partial_value, jax.lax.psum(1, 'na...  53.1 us
    all_to_all x4, waiting for transfers between devices, per_device(): lax.all_to_all(second, 'narrow', split_axis=0, concat_axis=1, tiled=True)  52 us
    all_to_all x4, starting transfers between devices, per_device(): lax.all_to_all(second, 'narrow', split_axis=0, concat_axis=1, tiled=True)  26.6 us
    convert_element_type x4, local copies, waits for them, and re-layouts, two_legs(): jnp.einsum('pb,abq->paq', op_b, first, preferred_element_type=jnp.float32)  16.6 us
    dot_general x4, matrix products, two_legs(): jnp.einsum('pb,abq->paq', op_b, first, preferred_element_type=jnp.float32)  15.8 us
    all_to_all x4, local copies, waits for them, and re-layouts, per_device(): lax.all_to_all(second, 'narrow', split_axis=0, concat_axis=1, tiled=True)  11.4 us
  transfers between devices with their start and end apart: 5, of which 5 were waited for; matrix products, arithmetic and copies ran while one was open for 8% of the time, Pallas kernels for 0%

profile of v1, /device:TPU:8, one launch (start us, length us, event | category | flops | bytes accessed | tf_op | source)
XLA Modules:
  0.0 458.7 jit_solution(5560028829223326391)
XLA Ops:
  6.5 1.8 fusion.115
  12.2 4.5 fusion.26
  16.7 4.2 copy.15
  20.9 6.3 %all-to-all-start.2 = ((bf16[256,16,256]{2,1,0:T(8,128)(2,1)}), bf16[256,16,256]{2,1,0:T(8,128)(2,1)}, u32[]{:S(2)}, u32[]{:S(2)}) async-start(bf16[256,16,256]{2,1,0:T(8,128)(2,1)} %copy.15), calls=%async_computation.2 | async-start | bytes 4194304 | tf_op jit(solution)/shard_map/all_to_all | solution.py:34
  31.3 3.8 fusion.23
  35.0 4.1 copy.13
  39.1 15.2 %all-to-all-done.2 = bf16[256,16,256]{2,1,0:T(8,128)(2,1)} async-done(((bf16[256,16,256]{2,1,0:T(8,128)(2,1)}), bf16[256,16,256]{2,1,0:T(8,128)(2,1)}, u32[]{:S(2)}, u32[]{:S(2)}) %all-to-all-start.2) | async-done | bytes 2097184 | tf_op jit(solution)/shard_map/all_to_all | solution.py:34
  54.4 6.8 %all-to-all-start.1 = ((bf16[256,16,256]{2,1,0:T(8,128)(2,1)}), bf16[256,16,256]{2,1,0:T(8,128)(2,1)}, u32[]{:S(2)}, u32[]{:S(2)}) async-start(bf16[256,16,256]{2,1,0:T(8,128)(2,1)} %copy.13), calls=%async_computation.1 | async-start | bytes 4194304 | tf_op jit(solution)/shard_map/all_to_all | solution.py:34
  64.9 3.8 fusion.20
  68.7 4.1 copy.11
  72.8 15.5 %all-to-all-done.1 = bf16[256,16,256]{2,1,0:T(8,128)(2,1)} async-done(((bf16[256,16,256]{2,1,0:T(8,128)(2,1)}), bf16[256,16,256]{2,1,0:T(8,128)(2,1)}, u32[]{:S(2)}, u32[]{:S(2)}) %all-to-all-start.1) | async-done | bytes 2097184 | tf_op jit(solution)/shard_map/all_to_all | solution.py:34
  88.3 6.8 %all-to-all-start = ((bf16[256,16,256]{2,1,0:T(8,128)(2,1)}), bf16[256,16,256]{2,1,0:T(8,128)(2,1)}, u32[]{:S(2)}, u32[]{:S(2)}) async-start(bf16[256,16,256]{2,1,0:T(8,128)(2,1)} %copy.11), calls=%async_computation | async-start | bytes 4194304 | tf_op jit(solution)/shard_map/all_to_all | solution.py:34
  98.7 3.8 fusion.29
  102.4 4.1 copy.17
  106.6 15.7 %all-to-all-done = bf16[256,16,256]{2,1,0:T(8,128)(2,1)} async-done(((bf16[256,16,256]{2,1,0:T(8,128)(2,1)}), bf16[256,16,256]{2,1,0:T(8,128)(2,1)}, u32[]{:S(2)}, u32[]{:S(2)}) %all-to-all-start) | async-done | bytes 2097184 | tf_op jit(solution)/shard_map/all_to_all | solution.py:34
  122.3 6.8 %all-to-all-start.3 = ((bf16[256,16,256]{2,1,0:T(8,128)(2,1)}), bf16[256,16,256]{2,1,0:T(8,128)(2,1)}, u32[]{:S(2)}, u32[]{:S(2)}) async-start(bf16[256,16,256]{2,1,0:T(8,128)(2,1)} %copy.17), calls=%async_computation.3 | async-start | bytes 4194304 | tf_op jit(solution)/shard_map/all_to_all | solution.py:34
  129.3 0.7 fusion.116
  140.1 1.1 dynamic-slice_bitcast_fusion
  141.2 3.1 copy.16
  144.4 3.1 copy.14
  147.5 3.1 copy.12
  150.7 5.6 %all-to-all-done.3 = bf16[256,16,256]{2,1,0:T(8,128)(2,1)} async-done(((bf16[256,16,256]{2,1,0:T(8,128)(2,1)}), bf16[256,16,256]{2,1,0:T(8,128)(2,1)}, u32[]{:S(2)}, u32[]{:S(2)}) %all-to-all-start.3) | async-done | bytes 2097184 | tf_op jit(solution)/shard_map/all_to_all | solution.py:34
  156.3 1.9 copy.18
  158.5 0.9 fusion.53
  159.4 0.5 copy-done.2
  159.9 0.9 fusion.57
  161.1 0.9 fusion.61
  162.0 1.1 add_add_fusion
  163.5 53.1 %all_to_all.77 = f32[16,16,16,256]{3,1,2,0:T(8,128)S(1)} all-to-all(f32[16,16,16,256]{3,1,2,0:T(8,128)S(1)} %fusion.32), channel_id=1, replica_groups=mesh['wide'=16,'narrow'=16] {'narrow'}, dimensions={0} | all-to-all | bytes 8388608 | tf_op jit(solution)/shard_map/all_to_all | solution.py:38
  216.6 4.4 copy.19
  221.1 225.0 %all-reduce.2.cloned.1.call-done = f32[16,256,256]{2,1,0:T(8,128)} async-done(((f32[16,256,256]{2,1,0:T(8,128)}), f32[16,256,256]{2,1,0:T(8,128)}) %all-reduce.2.cloned.1.call-update) | async-done | bytes 4194320 | tf_op jit(solution)/shard_map/psum | solution.py:43
  446.1 5.7 %multiply_add_fusion = f32[16,256,256]{2,1,0:T(8,128)} fusion(f32[16,256,256]{2,1,0:T(8,128)} %all-reduce.2.cloned.1.call-done, bf16[16,256,256]{2,1,0:T(8,128)(2,1)} %param.8, bf16[16,256,256]{2,1,0:T(8,128)(2,1)S(1)} %copy-done), kind=kLoop, calls=%fused_computation | loop fusion | flops 5242880 | bytes 12582912 | tf_op jit(solution)/shard_map/add | solution.py:44
  (27 shorter events, 1.2 us)
Async XLA Ops:
  16.7 14.5 %copy-start = (bf16[16,256,256]{2,1,0:T(8,128)(2,1)S(1)}, bf16[16,256,256]{2,1,0:T(8,128)(2,1)}, u32[]{:S(2)}) copy-start(bf16[16,256,256]{2,1,0:T(8,128)(2,1)} %param.7) | copy-start | bytes 6291460
  20.9 33.4 %all-to-all-start.2 = ((bf16[256,16,256]{2,1,0:T(8,128)(2,1)}), bf16[256,16,256]{2,1,0:T(8,128)(2,1)}, u32[]{:S(2)}, u32[]{:S(2)}) async-start(bf16[256,16,256]{2,1,0:T(8,128)(2,1)} %copy.15), calls=%async_computation.2 | async-start | bytes 4194304 | tf_op jit(solution)/shard_map/all_to_all | solution.py:34
  54.4 34.0 %all-to-all-start.1 = ((bf16[256,16,256]{2,1,0:T(8,128)(2,1)}), bf16[256,16,256]{2,1,0:T(8,128)(2,1)}, u32[]{:S(2)}, u32[]{:S(2)}) async-start(bf16[256,16,256]{2,1,0:T(8,128)(2,1)} %copy.13), calls=%async_computation.1 | async-start | bytes 4194304 | tf_op jit(solution)/shard_map/all_to_all | solution.py:34
  88.3 34.0 %all-to-all-start = ((bf16[256,16,256]{2,1,0:T(8,128)(2,1)}), bf16[256,16,256]{2,1,0:T(8,128)(2,1)}, u32[]{:S(2)}, u32[]{:S(2)}) async-start(bf16[256,16,256]{2,1,0:T(8,128)(2,1)} %copy.11), calls=%async_computation | async-start | bytes 4194304 | tf_op jit(solution)/shard_map/all_to_all | solution.py:34
  102.4 26.8 %copy-start.4 = (s32[4]{0:T(128)S(1)}, s32[4]{0:T(128)}, u32[]{:S(2)}) copy-start(s32[4]{0:T(128)} %param.11) | copy-start | bytes 52
  122.3 34.0 %all-to-all-start.3 = ((bf16[256,16,256]{2,1,0:T(8,128)(2,1)}), bf16[256,16,256]{2,1,0:T(8,128)(2,1)}, u32[]{:S(2)}, u32[]{:S(2)}) async-start(bf16[256,16,256]{2,1,0:T(8,128)(2,1)} %copy.17), calls=%async_computation.3 | async-start | bytes 4194304 | tf_op jit(solution)/shard_map/all_to_all | solution.py:34
  129.1 317.0 %all-reduce.2.cloned.1.call-start = ((), (), s32[]{:S(2)}) async-start(), calls=%async_computation.5 | async-start | bytes 8388608 | tf_op jit(solution)/shard_map/psum | solution.py:43
  156.3 2.2 copy-start.3
  158.2 1.7 copy-start.2
  159.4 1.7 copy-start.1
Sparse Core Ops, SparseCore 0:
  221.2 224.8 all-reduce.1
